TPU v7x, 32 devices: a whole 2x2x4 slice. The times are simulated.
32 devices in a mesh: dp: 4 (over y, x), tensor: 8 (over z, core).
Axes of the slice: x: 2, y: 2, z: 4, core: 2. Of those that a mesh axis runs over, the one named last changes fastest.
Arguments:
- inputs: bfloat16 [16384, 2048], P(('dp', 'tensor')), may hold values from -6 to 6
- block_ids: int32 [16, 1024], P('dp'), may hold values from 0 to 4, never falling along the last dimension, each value on 1 to 256 neighbouring positions
- norm_gain: bfloat16 [2048], replicated, may hold values from 0.5 to 1.5
- norm_bias: bfloat16 [2048], replicated, may hold values from -3 to 3
- query_weight: bfloat16 [2048, 2048], P('dp', 'tensor'), may hold values from -0.125 to 0.125
- query_bias: bfloat16 [2048], P('tensor'), may hold values from -3 to 3
- key_weight: bfloat16 [2048, 2048], P('dp', 'tensor'), may hold values from -0.125 to 0.125
- key_bias: bfloat16 [2048], P('tensor'), may hold values from -3 to 3
- value_weight: bfloat16 [2048, 2048], P('dp', 'tensor'), may hold values from -0.125 to 0.125
- value_bias: bfloat16 [2048], P('tensor'), may hold values from -3 to 3
- out_weight: bfloat16 [2048, 2048], P('tensor', 'dp'), may hold values from -3 to 3
- out_bias: bfloat16 [2048], replicated, may hold values from -3 to 3
- up_weight: bfloat16 [2048, 8192], P('dp', 'tensor'), may hold values from -0.125 to 0.125
- up_bias: bfloat16 [8192], P('tensor'), may hold values from -3 to 3
- down_weight: bfloat16 [8192, 2048], P('tensor', 'dp'), may hold values from -0.09375 to 0.09375
- down_bias: bfloat16 [2048], replicated, may hold values from -3 to 3
- grad_out: bfloat16 [16384, 2048], P(('dp', 'tensor')), may hold values from -6 to 6
Outputs:
- output: bfloat16 [16384, 2048], P(('dp', 'tensor'))
- input_grad: bfloat16 [16384, 2048], P(('dp', 'tensor'))
- norm_gain_grad: float32 [2048], replicated
- norm_bias_grad: float32 [2048], replicated
- query_weight_grad: float32 [2048, 2048], P('dp', 'tensor')
- query_bias_grad: float32 [2048], P('tensor')
- key_weight_grad: float32 [2048, 2048], P('dp', 'tensor')
- key_bias_grad: float32 [2048], P('tensor')
- value_weight_grad: float32 [2048, 2048], P('dp', 'tensor')
- value_bias_grad: float32 [2048], P('tensor')
- out_weight_grad: float32 [2048, 2048], P('tensor', 'dp')
- out_bias_grad: float32 [2048], replicated
- up_weight_grad: float32 [2048, 8192], P('dp', 'tensor')
- up_bias_grad: float32 [8192], P('tensor')
- down_weight_grad: float32 [8192, 2048], P('tensor', 'dp')
- down_bias_grad: float32 [2048], replicated
Inputs may be any that keep to these rules, and one draw needn't show every extreme that they name: `block_ids`: in each sequence the block numbers never fall along the positions; a block spans 1 to 256 positions, and one block of each sequence spans exactly 256.
All inputs are finite; a program needn't handle non-finite values.
Results may differ from a plain program's by a relative error of at most 0.012.
The roundings to bfloat16 on the way count: a program that leaves them out, or rounds other values in their place, can miss the bound.
Values may be sent and summed in bfloat16 or wider, within the bound.
A program may use at most 320 MiB of HBM per device.

v0:
```python
import jax
import jax.numpy as jnp
from jax import lax
from jax.sharding import PartitionSpec as P

HEAD_DIM = 64
ROT = 32
eps_norm = 1e-05


def normalize(values, gain_in, shift_in):
    center = jnp.mean(values, axis=-1, keepdims=True)
    centered = values - center
    variance = jnp.mean(centered * centered, axis=-1, keepdims=True)
    return centered * lax.rsqrt(variance + eps_norm) * gain_in + shift_in


def rotary_tables(length, rot_width):
    halves = rot_width // 2
    exponent = jnp.arange(halves, dtype=jnp.float32) * (2.0 / rot_width)
    frequency = jnp.power(10000.0, -exponent)
    angles = jnp.arange(length, dtype=jnp.float32)[:, None] * frequency[None, :]
    angles = jnp.concatenate([angles, angles], axis=1)
    return (jnp.cos(angles), jnp.sin(angles))


def rotate(per_head, cos_table, sin_table):
    rot_width = cos_table.shape[-1]
    halves = rot_width // 2
    first_half = per_head[..., :halves]
    second_half = per_head[..., halves:rot_width]
    turned = jnp.concatenate([-second_half, first_half], axis=-1)
    rotated = per_head[..., :rot_width] * cos_table[:, None, :] + turned * sin_table[:, None, :]
    return jnp.concatenate([rotated, per_head[..., rot_width:]], axis=-1)


def masked_scores(query_block, key_block, query_ids, key_ids):
    raw_scores = jnp.einsum(
        "qhd,khd->hqk", query_block, key_block, preferred_element_type=jnp.float32
    ) * HEAD_DIM ** (-0.5)
    allowed = key_ids[None, None, :] <= query_ids[None, :, None]
    return jnp.where(allowed, raw_scores, -1000000000.0)


def gelu_tanh(values):
    return jax.nn.gelu(values, approximate=True)


def per_device(
    inputs,
    block_ids,
    norm_gain,
    norm_bias,
    query_weight,
    query_bias,
    key_weight,
    key_bias,
    value_weight,
    value_bias,
    out_weight,
    out_bias,
    up_weight,
    up_bias,
    down_weight,
    down_bias,
    grad_out,
):
    seq_count, length = block_ids.shape
    local_width = query_weight.shape[1]
    local_heads = local_width // HEAD_DIM
    block_rows = min(512, length)
    per_sequence = length // block_rows
    all_rows = seq_count * length
    score_scale = HEAD_DIM ** (-0.5)
    gain_float = norm_gain.astype(jnp.float32)
    shift_float = norm_bias.astype(jnp.float32)
    inputs_float = inputs.astype(jnp.float32)
    normed = normalize(inputs_float, gain_float, shift_float).astype(jnp.bfloat16)
    full_query, full_key, full_value, full_up, full_out, full_down = (
        lax.all_gather(query_weight, "dp", axis=0, tiled=True),
        lax.all_gather(key_weight, "dp", axis=0, tiled=True),
        lax.all_gather(value_weight, "dp", axis=0, tiled=True),
        lax.all_gather(up_weight, "dp", axis=0, tiled=True),
        lax.all_gather(out_weight, "dp", axis=1, tiled=True),
        lax.all_gather(down_weight, "dp", axis=1, tiled=True),
    )
    group_rows = lax.all_gather(normed, "tensor", axis=0, tiled=True)
    cos_table, sin_table = rotary_tables(length, ROT)

    def project(weight_part, bias_part):
        return jnp.dot(
            group_rows, weight_part, preferred_element_type=jnp.float32
        ) + bias_part.astype(jnp.float32)

    def split_heads(values):
        return values.reshape(seq_count, length, local_heads, HEAD_DIM)

    queries = rotate(split_heads(project(full_query, query_bias)), cos_table, sin_table).astype(
        jnp.bfloat16
    )
    key_rows = rotate(split_heads(project(full_key, key_bias)), cos_table, sin_table).astype(
        jnp.bfloat16
    )
    value_rows = split_heads(project(full_value, value_bias)).astype(jnp.bfloat16)

    def forward_block(block_index):
        sequence = block_index // per_sequence
        offset = block_index % per_sequence * block_rows
        seq_ids = block_ids[sequence]
        query_block = lax.dynamic_slice_in_dim(queries[sequence], offset, block_rows, 0)
        query_ids = lax.dynamic_slice_in_dim(seq_ids, offset, block_rows, 0)
        scores = masked_scores(query_block, key_rows[sequence], query_ids, seq_ids)
        highest = jnp.max(scores, axis=2, keepdims=True)
        shifted = jnp.exp(scores - highest)
        totals = jnp.sum(shifted, axis=2, keepdims=True)
        weights_low = (shifted / totals).astype(jnp.bfloat16)
        mixed_rows = jnp.einsum(
            "hqk,khd->qhd", weights_low, value_rows[sequence], preferred_element_type=jnp.float32
        )
        return (mixed_rows, (highest + jnp.log(totals))[:, :, 0])

    attended, log_sums = lax.map(forward_block, jnp.arange(seq_count * per_sequence))
    attended_low = attended.reshape(all_rows, local_width).astype(jnp.bfloat16)
    hidden = project(full_up, up_bias)
    active = gelu_tanh(hidden).astype(jnp.bfloat16)
    branch_rows = lax.psum_scatter(
        jnp.dot(attended_low, full_out, preferred_element_type=jnp.float32)
        + jnp.dot(active, full_down, preferred_element_type=jnp.float32),
        "tensor",
        scatter_dimension=0,
        tiled=True,
    )
    output = (
        inputs_float + branch_rows + out_bias.astype(jnp.float32) + down_bias.astype(jnp.float32)
    ).astype(jnp.bfloat16)
    back_query, back_key, back_value, back_up, back_out, back_down = (
        lax.all_gather(query_weight, "dp", axis=0, tiled=True),
        lax.all_gather(key_weight, "dp", axis=0, tiled=True),
        lax.all_gather(value_weight, "dp", axis=0, tiled=True),
        lax.all_gather(up_weight, "dp", axis=0, tiled=True),
        lax.all_gather(out_weight, "dp", axis=1, tiled=True),
        lax.all_gather(down_weight, "dp", axis=1, tiled=True),
    )
    back_rows = lax.all_gather(normed, "tensor", axis=0, tiled=True)
    upstream = lax.all_gather(grad_out, "tensor", axis=0, tiled=True)
    out_wgrad = jnp.einsum("rk,rd->kd", attended_low, upstream, preferred_element_type=jnp.float32)
    down_wgrad = jnp.einsum("rf,rd->fd", active, upstream, preferred_element_type=jnp.float32)
    attended_grad = jnp.einsum(
        "rd,kd->rk", upstream, back_out, preferred_element_type=jnp.float32
    ).astype(jnp.bfloat16)
    active_grad = jnp.einsum("rd,fd->rf", upstream, back_down, preferred_element_type=jnp.float32)
    unused_value, gelu_pull = jax.vjp(gelu_tanh, hidden)
    hidden_grad = gelu_pull(active_grad)[0].astype(jnp.bfloat16)
    grad_heads = split_heads(attended_grad)
    sums_grouped = log_sums.reshape(seq_count, per_sequence, local_heads, block_rows)

    def backward_sequence(sequence):
        seq_ids = block_ids[sequence]
        seq_queries = queries[sequence]
        seq_keys = key_rows[sequence]
        seq_values = value_rows[sequence]
        seq_grads = grad_heads[sequence]
        seq_sums = sums_grouped[sequence]

        def backward_block(running, block_number):
            key_total, value_total = running
            offset = block_number * block_rows
            query_block = lax.dynamic_slice_in_dim(seq_queries, offset, block_rows, 0)
            query_ids = lax.dynamic_slice_in_dim(seq_ids, offset, block_rows, 0)
            grad_block = lax.dynamic_slice_in_dim(seq_grads, offset, block_rows, 0)
            scores = masked_scores(query_block, seq_keys, query_ids, seq_ids)
            prob_rows = jnp.exp(scores - seq_sums[block_number][:, :, None])
            value_total = value_total + jnp.einsum(
                "hqk,qhd->khd",
                prob_rows.astype(jnp.bfloat16),
                grad_block,
                preferred_element_type=jnp.float32,
            )
            prob_grad = jnp.einsum(
                "qhd,khd->hqk", grad_block, seq_values, preferred_element_type=jnp.float32
            )
            row_inner = jnp.sum(prob_grad * prob_rows, axis=2, keepdims=True)
            score_grad = (prob_rows * (prob_grad - row_inner)).astype(jnp.bfloat16)
            query_part = (
                jnp.einsum("hqk,khd->qhd", score_grad, seq_keys, preferred_element_type=jnp.float32)
                * score_scale
            )
            key_total = (
                key_total
                + jnp.einsum(
                    "hqk,qhd->khd", score_grad, query_block, preferred_element_type=jnp.float32
                )
                * score_scale
            )
            return ((key_total, value_total), query_part)

        zero_total = jnp.zeros((length, local_heads, HEAD_DIM), jnp.float32)
        (key_total, value_total), query_parts = lax.scan(
            backward_block, (zero_total, zero_total), jnp.arange(per_sequence)
        )
        return (query_parts.reshape(length, local_heads, HEAD_DIM), key_total, value_total)

    query_grad_rot, key_grad_rot, value_grad_all = lax.map(backward_sequence, jnp.arange(seq_count))
    query_grad = (
        rotate(query_grad_rot, cos_table, -sin_table)
        .reshape(all_rows, local_width)
        .astype(jnp.bfloat16)
    )
    key_grad = (
        rotate(key_grad_rot, cos_table, -sin_table)
        .reshape(all_rows, local_width)
        .astype(jnp.bfloat16)
    )
    value_grad = value_grad_all.reshape(all_rows, local_width).astype(jnp.bfloat16)
    query_wgrad = jnp.einsum("rd,rk->dk", back_rows, query_grad, preferred_element_type=jnp.float32)
    key_wgrad = jnp.einsum("rd,rk->dk", back_rows, key_grad, preferred_element_type=jnp.float32)
    value_wgrad = jnp.einsum("rd,rk->dk", back_rows, value_grad, preferred_element_type=jnp.float32)
    up_wgrad = jnp.einsum("rd,rf->df", back_rows, hidden_grad, preferred_element_type=jnp.float32)
    normed_grad = lax.psum_scatter(
        jnp.einsum("rk,dk->rd", query_grad, back_query, preferred_element_type=jnp.float32)
        + jnp.einsum("rk,dk->rd", key_grad, back_key, preferred_element_type=jnp.float32)
        + jnp.einsum("rk,dk->rd", value_grad, back_value, preferred_element_type=jnp.float32)
        + jnp.einsum("rf,df->rd", hidden_grad, back_up, preferred_element_type=jnp.float32),
        "tensor",
        scatter_dimension=0,
        tiled=True,
    )
    unused_norm, norm_pull = jax.vjp(normalize, inputs_float, gain_float, shift_float)
    input_part, gain_part, shift_part = norm_pull(normed_grad)
    input_grad = (grad_out.astype(jnp.float32) + input_part).astype(jnp.bfloat16)
    bias_part = jnp.sum(grad_out, axis=0, dtype=jnp.float32)
    gain_grad, shift_grad, outer_bias_grad = lax.psum(
        (gain_part, shift_part, bias_part), ("dp", "tensor")
    )
    query_bias_grad, key_bias_grad, value_bias_grad, up_bias_grad = lax.psum(
        (
            jnp.sum(query_grad, axis=0, dtype=jnp.float32),
            jnp.sum(key_grad, axis=0, dtype=jnp.float32),
            jnp.sum(value_grad, axis=0, dtype=jnp.float32),
            jnp.sum(hidden_grad, axis=0, dtype=jnp.float32),
        ),
        "dp",
    )
    (
        query_weight_grad,
        key_weight_grad,
        value_weight_grad,
        up_weight_grad,
        out_weight_grad,
        down_weight_grad,
    ) = (
        lax.psum_scatter(query_wgrad, "dp", scatter_dimension=0, tiled=True),
        lax.psum_scatter(key_wgrad, "dp", scatter_dimension=0, tiled=True),
        lax.psum_scatter(value_wgrad, "dp", scatter_dimension=0, tiled=True),
        lax.psum_scatter(up_wgrad, "dp", scatter_dimension=0, tiled=True),
        lax.psum_scatter(out_wgrad, "dp", scatter_dimension=1, tiled=True),
        lax.psum_scatter(down_wgrad, "dp", scatter_dimension=1, tiled=True),
    )
    return (
        output,
        input_grad,
        gain_grad,
        shift_grad,
        query_weight_grad,
        query_bias_grad,
        key_weight_grad,
        key_bias_grad,
        value_weight_grad,
        value_bias_grad,
        out_weight_grad,
        outer_bias_grad,
        up_weight_grad,
        up_bias_grad,
        down_weight_grad,
        outer_bias_grad,
    )


def solution(mesh):
    return jax.shard_map(
        per_device,
        mesh=mesh,
        in_specs=(
            P(("dp", "tensor"), None),
            P("dp", None),
            P(),
            P(),
            P("dp", "tensor"),
            P("tensor"),
            P("dp", "tensor"),
            P("tensor"),
            P("dp", "tensor"),
            P("tensor"),
            P("tensor", "dp"),
            P(),
            P("dp", "tensor"),
            P("tensor"),
            P("tensor", "dp"),
            P(),
            P(("dp", "tensor"), None),
        ),
        out_specs=(
            P(("dp", "tensor"), None),
            P(("dp", "tensor"), None),
            P(),
            P(),
            P("dp", "tensor"),
            P("tensor"),
            P("dp", "tensor"),
            P("tensor"),
            P("dp", "tensor"),
            P("tensor"),
            P("tensor", "dp"),
            P(),
            P("dp", "tensor"),
            P("tensor"),
            P("tensor", "dp"),
            P(),
        ),
        check_vma=False,
    )
```

profile of v0, /device:TPU:0, one launch (start us, length us, event | category | flops | bytes accessed | tf_op | source)
XLA Modules:
  0.0 2073.4 jit_solution(4787446761198307838)
XLA Ops:
  22.7 16.5 all-gather.15.cloned.1.call-done
  39.2 153.3 %all-gather.9.cloned.1.call-done = bf16[4096,2048]{1,0:T(8,128)(2,1)} async-done(((bf16[512,2048]{1,0:T(8,128)(2,1)}), bf16[4096,2048]{1,0:T(8,128)(2,1)}) %all-gather.9.cloned.1.call-update) | async-done | bytes 16777232 | tf_op jit(solution)/shard_map/all_gather | solution.py:87
  278.6 149.8 %all-gather.23.cloned.1.call-done = bf16[4096,2048]{1,0:T(8,128)(2,1)} async-done(((bf16[512,2048]{1,0:T(8,128)(2,1)}), bf16[4096,2048]{1,0:T(8,128)(2,1)}) %all-gather.23.cloned.1.call-update) | async-done | bytes 16777232 | tf_op jit(solution)/shard_map/all_gather | solution.py:145
  466.2 102.8 %while.44 = (s32[]{:T(128)}, bf16[8,512,4,64]{1,3,2,0:T(8,128)(2,1)S(1)}, f32[8,4,512]{2,1,0:T(4,128)S(1)}, s32[8]{0:T(128)S(1)}, bf16[4,1024,4,64]{1,3,2,0:T(8,...) while((s32[]{:T(128)}, ...), condition=%wide.region_5.6_spmd, body=%wide.region_2.5_spmd.sunk | while | flops 562558976 | bytes 29182452 | solution.py:122
  570.3 342.7 %while.46 = (s32[]{:T(128)}, f32[4,1024,4,64]{1,0,3,2:T(4,128)}, f32[4,1024,4,64]{1,0,3,2:T(4,128)}, bf16[4,1024,4,64]{1,3,2,0:T(8,128)(2,1)}, s32[4]{0:T(128)S(...) while((s32[]{:T(128)}, f32[4,1024,4,64]{1,0,3,2:T(4,128)}, ...), condition=%wide.region_11.12_spmd, body=%wide.region_7.11_spmd.sunk | while | flops 1375598592 | bytes 110209856 | solution.py:203
  575.7 33.3 %while.47 = (s32[]{:T(128)}, f32[1024,4,64]{0,2,1:T(8,128)S(1)}, f32[1024,4,64]{0,2,1:T(8,128)}, f32[2,512,4,64]{1,3,2,0:T(8,128)}, s32[2]{0:T(128)S(1)}, /*inde...) while((s32[]{:T(128)}, f32[1024,4,64]{0,2,1:T(8,128)S(1)}, ...), condition=%wide.region_10.10_spmd.clone, body=%wide.region_8.9_spmd.clone.sunk | while | flops 1375598592 | bytes 89196952 | solution.py:198
  616.2 19.9 dynamic_update_slice.44
  636.1 19.9 dynamic_update_slice.45
  661.3 33.3 %while.47 = (s32[]{:T(128)}, f32[1024,4,64]{0,2,1:T(8,128)S(1)}, f32[1024,4,64]{0,2,1:T(8,128)}, f32[2,512,4,64]{1,3,2,0:T(8,128)}, s32[2]{0:T(128)S(1)}, /*inde...) while((s32[]{:T(128)}, f32[1024,4,64]{0,2,1:T(8,128)S(1)}, ...), condition=%wide.region_10.10_spmd.clone, body=%wide.region_8.9_spmd.clone.sunk | while | flops 1375598592 | bytes 89196952 | solution.py:198
  701.8 19.9 dynamic_update_slice.44
  721.7 19.9 dynamic_update_slice.45
  746.9 33.3 %while.47 = (s32[]{:T(128)}, f32[1024,4,64]{0,2,1:T(8,128)S(1)}, f32[1024,4,64]{0,2,1:T(8,128)}, f32[2,512,4,64]{1,3,2,0:T(8,128)}, s32[2]{0:T(128)S(1)}, /*inde...) while((s32[]{:T(128)}, f32[1024,4,64]{0,2,1:T(8,128)S(1)}, ...), condition=%wide.region_10.10_spmd.clone, body=%wide.region_8.9_spmd.clone.sunk | while | flops 1375598592 | bytes 89196952 | solution.py:198
  787.4 19.9 dynamic_update_slice.44
  807.3 19.9 dynamic_update_slice.45
  832.5 33.3 %while.47 = (s32[]{:T(128)}, f32[1024,4,64]{0,2,1:T(8,128)S(1)}, f32[1024,4,64]{0,2,1:T(8,128)}, f32[2,512,4,64]{1,3,2,0:T(8,128)}, s32[2]{0:T(128)S(1)}, /*inde...) while((s32[]{:T(128)}, f32[1024,4,64]{0,2,1:T(8,128)S(1)}, ...), condition=%wide.region_10.10_spmd.clone, body=%wide.region_8.9_spmd.clone.sunk | while | flops 1375598592 | bytes 89196952 | solution.py:198
  873.0 19.9 dynamic_update_slice.44
  892.9 19.9 dynamic_update_slice.45
  942.3 13.5 fusion.82
  972.8 23.4 %fusion.80 = f32[4096,1024]{1,0:T(8,128)} fusion(bf16[4096,2048]{1,0:T(8,128)(2,1)} %all-gather.9.cloned.1.call-done, bf16[2048,1024]{1,0:T(8,128)(2,1)} %all-gather.19.cloned.1.call-done), kind=kOutput, calls=%fused_computation.136 | convolution fusion | flops 17179869184 | bytes 37748736 | tf_op jit(solution)/shard_map/dot_general | solution.py:91
  996.2 36.5 %convert_reduce_fusion = (f32[1024]{0:T(1024)}, bf16[4096,1024]{1,0:T(8,128)(2,1)}) fusion(f32[4096,1024]{1,0:T(8,128)} %fusion.80, f32[1024]{0:T(1024)S(1)} %copy-done.40, bf16[4096,2048]{1,0:T(8,128)(2,1)} %all-gather.23.cloned.1.call-done, bf16[1024,2048]{1,0:T(8,128)(2,1)} %all-gather.21.cloned.1.call-done), kind=kOutput, calls=%fused_computation.68 | convolution fusion | flops 17276338176 | bytes 46145536 | tf_op jit(solution)/shard_map/rd,fd->rf/dot_general | solution.py:151
  1032.6 48.6 %add_add_fusion = f32[4096,2048]{1,0:T(8,128)} fusion(f32[4096,2048]{1,0:T(8,128)} %fusion.83, f32[4096,2048]{1,0:T(8,128)} %fusion.81, f32[4096,2048]{1,0:T(8,128)} %fusion.82, bf16[4096,1024]{1,0:T(8,128)(2,1)} %get-tuple-element.433, bf16[2048,1024]{1,0:T(8,128)(2,1)} %all-gather.19.cloned.1.call-done), kind=kOutput, calls=%fused_computation.57 | convolution fusion | flops 17205035008 | bytes 146800640 | tf_op jit(solution)/shard_map/rf,df->rd/dot_general | solution.py:223
  1099.7 34.0 %convolution_add_fusion = f32[4096,2048]{1,0:T(8,128)} fusion(f32[4096,2048]{1,0:T(8,128)} %fusion.79, bf16[1024,2048]{1,0:T(8,128)(2,1)S(1)} %copy-done.42, f32[4096,1024]{1,0:T(8,128)} %fusion.80, f32[1024]{0:T(1024)S(1)} %copy-done.40), kind=kOutput, calls=%fused_computation.60 | convolution fusion | flops 17230200832 | bytes 88084480 | tf_op jit(solution)/shard_map/dot_general | solution.py:128
  1179.9 24.2 %fusion.88 = f32[2048,1024]{1,0:T(8,128)} fusion(bf16[4096,2048]{1,0:T(8,128)(2,1)} %all-gather.9.cloned.1.call-done, bf16[4096,1024]{1,0:T(8,128)(2,1)} %get-tuple-element.433), kind=kOutput, calls=%fused_computation.144 | convolution fusion | flops 17179869184 | bytes 33554432 | tf_op jit(solution)/shard_map/rd,rf->df/dot_general | solution.py:218
  1204.2 28.9 %fusion.76 = f32[1024,2048]{1,0:T(8,128)} fusion(bf16[4096,2048]{1,0:T(8,128)(2,1)} %all-gather.23.cloned.1.call-done, f32[4096,1024]{1,0:T(8,128)} %fusion.80, f32[1024]{0:T(1024)S(1)} %copy-done.40), kind=kOutput, calls=%fused_computation.133 | convolution fusion | flops 17221812224 | bytes 41947136 | tf_op jit(solution)/shard_map/rf,rd->fd/dot_general | solution.py:147
  1246.9 158.2 %reduce-scatter.11.cloned.1.call-done = f32[512,2048]{1,0:T(8,128)} async-done(((f32[4096,2048]{1,0:T(8,128)}), f32[512,2048]{1,0:T(8,128)}) %reduce-scatter.11.cloned.1.call-update) | async-done | bytes 4194320 | tf_op jit(solution)/shard_map/reduce_scatter | solution.py:219
  1410.6 320.8 %reduce-scatter.9.cloned.1.call-done = f32[512,2048]{1,0:T(8,128)} async-done(((f32[4096,2048]{1,0:T(8,128)}), f32[512,2048]{1,0:T(8,128)}) %reduce-scatter.9.cloned.1.call-update) | async-done | bytes 4194320 | tf_op jit(solution)/shard_map/reduce_scatter | solution.py:126
  1739.0 38.3 %all-reduce = (f32[2048]{0:T(1024)}, f32[2048]{0:T(1024)}, f32[2048]{0:T(1024)S(1)}) all-reduce(f32[2048]{0:T(1024)S(1)} %get-tuple-element.359, f32[2048]{0:T(1024)S(1)} %get-tuple-element.361, f32[2048]{0:T(1024)S(1)} %get-tuple-element.458), channel_id=1, replica_groups=mesh['dp'=4,'tensor'=8] {'dp','tensor'}, use_global_device_ids=true, to_apply=%region_16.17 | all-reduce | flops 6144 | bytes 49152 | tf_op jit(solution)/shard_map/psum | solution.py:232
  1777.3 30.9 %reduce-scatter.17.cloned.1.call-done = f32[512,256]{1,0:T(8,128)} async-done(((f32[2048,256]{1,0:T(8,128)}), f32[512,256]{1,0:T(8,128)}) %reduce-scatter.17.cloned.1.call-update) | async-done | bytes 524304 | tf_op jit(solution)/shard_map/reduce_scatter | solution.py:254
  1808.2 38.7 %reduce-scatter.15.cloned.1.call-done = f32[512,256]{1,0:T(8,128)} async-done(((f32[2048,256]{1,0:T(8,128)}), f32[512,256]{1,0:T(8,128)}) %reduce-scatter.15.cloned.1.call-update) | async-done | bytes 524304 | tf_op jit(solution)/shard_map/reduce_scatter | solution.py:253
  1847.0 38.9 %reduce-scatter.13.cloned.1.call-done = f32[512,256]{1,0:T(8,128)} async-done(((f32[2048,256]{1,0:T(8,128)}), f32[512,256]{1,0:T(8,128)}) %reduce-scatter.13.cloned.1.call-update) | async-done | bytes 524304 | tf_op jit(solution)/shard_map/reduce_scatter | solution.py:252
  1885.9 89.9 %reduce-scatter.21.cloned.1.call-done = f32[512,1024]{1,0:T(8,128)} async-done(((f32[2048,1024]{1,0:T(8,128)}), f32[512,1024]{1,0:T(8,128)}) %reduce-scatter.21.cloned.1.call-update) | async-done | bytes 2097168 | tf_op jit(solution)/shard_map/reduce_scatter | solution.py:255
  1975.8 90.2 %reduce-scatter.23.cloned.1.call-done = f32[1024,512]{1,0:T(8,128)} async-done(((f32[1024,2048]{1,0:T(8,128)}), f32[1024,512]{1,0:T(8,128)}) %reduce-scatter.23.cloned.1.call-update) | async-done | bytes 2097168 | tf_op jit(solution)/shard_map/reduce_scatter | solution.py:257
  (460 shorter events, 513.3 us)
Async XLA Ops:
  7.2 32.0 %all-gather.15.cloned.1.call-start = ((), (), s32[]{:S(2)}) async-start(), calls=%async_computation.11 | async-start | bytes 1310720 | tf_op jit(solution)/shard_map/all_gather | solution.py:81
  7.9 184.6 %all-gather.9.cloned.1.call-start = ((), (), s32[]{:S(2)}) async-start(), calls=%async_computation.8 | async-start | bytes 18874368 | tf_op jit(solution)/shard_map/all_gather | solution.py:87
  17.0 205.3 %all-gather.13.cloned.1.call-start = ((), (), s32[]{:S(2)}) async-start(), calls=%async_computation.10 | async-start | bytes 1310720 | tf_op jit(solution)/shard_map/all_gather | solution.py:80
  17.7 234.8 %all-gather.11.cloned.1.call-start = ((), (), s32[]{:S(2)}) async-start(), calls=%async_computation.9 | async-start | bytes 1310720 | tf_op jit(solution)/shard_map/all_gather | solution.py:82
  18.3 260.3 %all-gather.17.cloned.1.call-start = ((), (), s32[]{:S(2)}) async-start(), calls=%async_computation.12 | async-start | bytes 1310720 | tf_op jit(solution)/shard_map/all_gather | solution.py:84
  18.9 409.6 %all-gather.23.cloned.1.call-start = ((), (), s32[]{:S(2)}) async-start(), calls=%async_computation.16 | async-start | bytes 18874368 | tf_op jit(solution)/shard_map/all_gather | solution.py:145
  19.4 953.3 %all-gather.19.cloned.1.call-start = ((), (), s32[]{:S(2)}) async-start(), calls=%async_computation.13 | async-start | bytes 5242880 | tf_op jit(solution)/shard_map/all_gather | solution.py:83
  20.2 976.0 %all-gather.21.cloned.1.call-start = ((), (), s32[]{:S(2)}) async-start(), calls=%async_computation.14 | async-start | bytes 5242880 | tf_op jit(solution)/shard_map/all_gather | solution.py:85
  20.9 1384.2 %reduce-scatter.11.cloned.1.call-start = ((), (), s32[]{:S(2)}) async-start(), calls=%async_computation.17 | async-start | bytes 37748736 | tf_op jit(solution)/shard_map/reduce_scatter | solution.py:219
  22.7 432.1 %copy-start.20 = (f32[1024,32]{0,1:T(8,128)}, f32[1024,32]{0,1:T(8,128)S(1)}, u32[]{:S(2)}) copy-start(f32[1024,32]{0,1:T(8,128)S(1)} %get-tuple-element.467) | copy-start | bytes 393220
  614.1 22.1 %copy-start = (f32[1,1024,4,64]{1,0,3,2:T(1,128)S(1)}, f32[1,1024,4,64]{1,0,3,2:T(1,128)}, u32[]{:S(2)}) copy-start(f32[1,1024,4,64]{1,0,3,2:T(1,128)} %copy.103) | copy-start | bytes 3145732 | tf_op jit(solution)/shard_map/while
  699.6 22.1 %copy-start = (f32[1,1024,4,64]{1,0,3,2:T(1,128)S(1)}, f32[1,1024,4,64]{1,0,3,2:T(1,128)}, u32[]{:S(2)}) copy-start(f32[1,1024,4,64]{1,0,3,2:T(1,128)} %copy.103) | copy-start | bytes 3145732 | tf_op jit(solution)/shard_map/while
  785.2 22.1 %copy-start = (f32[1,1024,4,64]{1,0,3,2:T(1,128)S(1)}, f32[1,1024,4,64]{1,0,3,2:T(1,128)}, u32[]{:S(2)}) copy-start(f32[1,1024,4,64]{1,0,3,2:T(1,128)} %copy.103) | copy-start | bytes 3145732 | tf_op jit(solution)/shard_map/while
  870.8 22.1 %copy-start = (f32[1,1024,4,64]{1,0,3,2:T(1,128)S(1)}, f32[1,1024,4,64]{1,0,3,2:T(1,128)}, u32[]{:S(2)}) copy-start(f32[1,1024,4,64]{1,0,3,2:T(1,128)} %copy.103) | copy-start | bytes 3145732 | tf_op jit(solution)/shard_map/while
  925.2 17.1 copy-start.10
  942.3 13.6 copy-start.14
  972.8 23.4 %copy-start.40 = (f32[1024]{0:T(1024)S(1)}, f32[1024]{0:T(1024)}, u32[]{:S(2)}) copy-start(f32[1024]{0:T(1024)} %convert_element_type.123) | copy-start | bytes 12292
  1081.3 650.1 %reduce-scatter.9.cloned.1.call-start = ((), (), s32[]{:S(2)}) async-start(), calls=%async_computation.15 | async-start | bytes 37748736 | tf_op jit(solution)/shard_map/reduce_scatter | solution.py:126
  1086.3 13.4 copy-start.42
  1133.7 643.6 %reduce-scatter.19.cloned.1.call-start = ((), (), s32[]{:S(2)}) async-start(), calls=%async_computation.21 | async-start | bytes 2621440 | tf_op jit(solution)/shard_map/reduce_scatter | solution.py:256
  1146.3 661.9 %reduce-scatter.17.cloned.1.call-start = ((), (), s32[]{:S(2)}) async-start(), calls=%async_computation.20 | async-start | bytes 2621440 | tf_op jit(solution)/shard_map/reduce_scatter | solution.py:254
  1156.6 13.2 copy-start.9
  1156.6 690.4 %reduce-scatter.15.cloned.1.call-start = ((), (), s32[]{:S(2)}) async-start(), calls=%async_computation.19 | async-start | bytes 2621440 | tf_op jit(solution)/shard_map/reduce_scatter | solution.py:253
  1169.7 716.2 %reduce-scatter.13.cloned.1.call-start = ((), (), s32[]{:S(2)}) async-start(), calls=%async_computation.18 | async-start | bytes 2621440 | tf_op jit(solution)/shard_map/reduce_scatter | solution.py:252
  1179.7 796.2 %reduce-scatter.21.cloned.1.call-start = ((), (), s32[]{:S(2)}) async-start(), calls=%async_computation.22 | async-start | bytes 10485760 | tf_op jit(solution)/shard_map/reduce_scatter | solution.py:255
  1204.2 861.9 %reduce-scatter.23.cloned.1.call-start = ((), (), s32[]{:S(2)}) async-start(), calls=%async_computation.23 | async-start | bytes 10485760 | tf_op jit(solution)/shard_map/reduce_scatter | solution.py:257
  1233.1 172.1 %copy-start.2 = (bf16[512,2048]{1,0:T(8,128)(2,1)S(1)}, bf16[512,2048]{1,0:T(8,128)(2,1)}, u32[]{:S(2)}) copy-start(bf16[512,2048]{1,0:T(8,128)(2,1)} %param.23) | copy-start | bytes 6291460
  1233.1 172.0 %copy-start.26 = (f32[2048]{0:T(1024)S(1)}, f32[2048]{0:T(1024)}, u32[]{:S(2)}) copy-start(f32[2048]{0:T(1024)} %copy-done.25) | copy-start | bytes 24580
  1233.1 172.0 %copy-start.29 = (f32[512]{0:T(512)S(1)}, f32[512]{0:T(512)}, u32[]{:S(2)}) copy-start(f32[512]{0:T(512)} %copy-done.28) | copy-start | bytes 6148
  1233.8 174.7 %copy-start.33 = (f32[512]{0:T(512)S(1)}, f32[512]{0:T(512)}, u32[]{:S(2)}) copy-start(f32[512]{0:T(512)} %copy-done.32) | copy-start | bytes 6148
  1233.8 174.7 %copy-start.31 = (f32[512]{0:T(512)S(1)}, f32[512]{0:T(512)}, u32[]{:S(2)}) copy-start(f32[512]{0:T(512)} %copy-done.30) | copy-start | bytes 6148
  1777.3 289.3 %copy-start.36 = (f32[2048]{0:T(1024)}, f32[2048]{0:T(1024)S(1)}, u32[]{:S(2)}) copy-start(f32[2048]{0:T(1024)S(1)} %get-tuple-element.893) | copy-start | bytes 24580
  (61 other events, 172.0 us)
Sparse Core Ops, SparseCore 0:
  9.9 29.3 all-gather.14
  41.4 151.0 all-gather.8
  194.4 24.8 all-gather.12
  221.0 26.6 all-gather.10
  249.3 26.4 all-gather.16
  277.3 151.1 all-gather.22
  430.3 50.9 all-gather.18
  483.1 52.5 all-gather.20
  1081.4 323.6 reduce-scatter.10
  1407.5 323.8 reduce-scatter.8
  1735.0 34.3 reduce-scatter.18
  1773.0 35.1 reduce-scatter.16
  1811.8 35.1 reduce-scatter.14
  1850.7 35.2 reduce-scatter.12
  1889.4 86.3 reduce-scatter.20
  1979.6 86.3 reduce-scatter.22
where the time goes:
time: 2090 us; the launch traced here: 2070 us
  waiting for transfers between devices  1090 us (52%)
  matrix products  473 us (23%)
  local copies, waits for them, and re-layouts  297 us (14%)
  other arithmetic  95.4 us (5%)
  loops' own time  51.3 us (2%)
  blocking collectives  49.1 us (2%)
    reduce_scatter x1, waiting for transfers between devices, per_device(): lax.psum_scatter(jnp.dot(attended_low, full_out, preferred_element_type=j...  321 us
    dynamic_update_slice x20, local copies, waits for them, and re-layouts, per_device(): lax.map(backward_sequence, jnp.arange(seq_count))  181 us
    reduce_scatter x1, waiting for transfers between devices, per_device(): lax.psum_scatter(jnp.einsum('rk,dk->rd', query_grad, back_query, preferre...  158 us
    all_gather x1, waiting for transfers between devices, per_device(): group_rows = lax.all_gather(normed, 'tensor', axis=0, tiled=True)  153 us
    all_gather x1, waiting for transfers between devices, per_device(): upstream = lax.all_gather(grad_out, 'tensor', axis=0, tiled=True)  150 us
    reduce_scatter x1, waiting for transfers between devices, per_device(): lax.psum_scatter(down_wgrad, 'dp', scatter_dimension=1, tiled=True)  90.2 us
    reduce_scatter x1, waiting for transfers between devices, per_device(): lax.psum_scatter(up_wgrad, 'dp', scatter_dimension=0, tiled=True)  89.9 us
    dot_general x4, matrix products, project(): jnp.dot(group_rows, weight_part, preferred_element_type=jnp.float32)  60.7 us
  transfers between devices with their start and end apart: 16, of which 10 were waited for; matrix products, arithmetic and copies ran while one was open for 37% of the time, Pallas kernels for 0%

commit v1 on v0

--- a/solution.py
+++ b/solution.py
@@ -2,6 +2,7 @@
 import jax.numpy as jnp
 from jax import lax
 from jax.sharding import PartitionSpec as P
+from jax.lax import axis_index, axis_size, ppermute
 
 HEAD_DIM = 64
 ROT = 32
@@ -84,7 +85,28 @@
         lax.all_gather(out_weight, "dp", axis=1, tiled=True),
         lax.all_gather(down_weight, "dp", axis=1, tiled=True),
     )
-    group_rows = lax.all_gather(normed, "tensor", axis=0, tiled=True)
+    moved = axis_size("tensor")
+    x_new = axis_index("tensor")
+    piece_next, v1, e_next = (moved, x_new, normed.shape[0])
+    front = jnp.zeros(
+        [dd * piece_next if to_i == 0 else dd for to_i, dd in enumerate(normed.shape)], normed.dtype
+    )
+    group_rows = lax.dynamic_update_slice_in_dim(front, normed, v1 * e_next, axis=0)
+    s_next = then = normed
+    for t in range(1, piece_next // 2 + 1):
+        s_next = ppermute(
+            s_next, "tensor", [(to_i, (to_i + 1) % piece_next) for to_i in range(piece_next)]
+        )
+        group_rows = lax.dynamic_update_slice_in_dim(
+            group_rows, s_next, (v1 - t) % piece_next * e_next, axis=0
+        )
+        if 2 * t < piece_next:
+            then = ppermute(
+                then, "tensor", [(to_i, (to_i - 1) % piece_next) for to_i in range(piece_next)]
+            )
+            group_rows = lax.dynamic_update_slice_in_dim(
+                group_rows, then, (v1 + t) % piece_next * e_next, axis=0
+            )
     cos_table, sin_table = rotary_tables(length, ROT)
 
     def project(weight_part, bias_part):

time: 2090 us -> 1960 us (0.938)
  waiting for transfers between devices: 1090 us -> 935 us
  local copies, waits for them, and re-layouts: 297 us -> 320 us
    all_gather x1, waiting for transfers between devices: 153 us -> 0.02 us  [per_device(): back_rows = lax.all_gather(normed, 'tensor', axis=0, tiled=True)]
    all_gather x1, waiting for transfers between devices: 150 us -> 0.01 us  [per_device(): upstream = lax.all_gather(grad_out, 'tensor', axis=0, tiled=True)]
    ppermute x0 -> x7, waiting for transfers between devices: none -> 137 us  [the longest x4 136 us: per_device(): ppermute(s_next, 'tensor', [(to_i, (to_i + 1) % piece_next) for to_i in r...]
    reduce_scatter x1, waiting for transfers between devices: 30.9 us -> 0.02 us  [per_device(): lax.psum_scatter(value_wgrad, 'dp', scatter_dimension=0, tiled=True)]
    reduce_scatter x1, waiting for transfers between devices: 0.02 us -> 30.9 us  [per_device(): lax.psum_scatter(out_wgrad, 'dp', scatter_dimension=1, tiled=True)]
    reduce_scatter x1, waiting for transfers between devices: 158 us -> 184 us  [per_device(): lax.psum_scatter(jnp.einsum('rk,dk->rd', query_grad, back_query, preferre...]
  transfers between devices with their start and end apart: 16 -> 23, of which waited for: 10 -> 13; matrix products, arithmetic and copies ran while one was open for 37% -> 44% of each run, Pallas kernels for 0% -> 0%
where the time goes in v1:
time: 1960 us; the launch traced here: 1950 us
  waiting for transfers between devices  935 us (48%)
  matrix products  472 us (24%)
  local copies, waits for them, and re-layouts  320 us (16%)
  other arithmetic  87.6 us (4%)
  blocking collectives  53.6 us (3%)
  loops' own time  51.6 us (3%)
    reduce_scatter x1, waiting for transfers between devices, per_device(): lax.psum_scatter(jnp.dot(attended_low, full_out, preferred_element_type=j...  321 us
    reduce_scatter x1, waiting for transfers between devices, per_device(): lax.psum_scatter(jnp.einsum('rk,dk->rd', query_grad, back_query, preferre...  184 us
    dynamic_update_slice x20, local copies, waits for them, and re-layouts, per_device(): lax.map(backward_sequence, jnp.arange(seq_count))  181 us
    ppermute x4, waiting for transfers between devices, per_device(): ppermute(s_next, 'tensor', [(to_i, (to_i + 1) % piece_next) for to_i in r...  136 us
    reduce_scatter x1, waiting for transfers between devices, per_device(): lax.psum_scatter(down_wgrad, 'dp', scatter_dimension=1, tiled=True)  90.2 us
    reduce_scatter x1, waiting for transfers between devices, per_device(): lax.psum_scatter(up_wgrad, 'dp', scatter_dimension=0, tiled=True)  89.9 us
    dot_general x4, matrix products, project(): jnp.dot(group_rows, weight_part, preferred_element_type=jnp.float32)  62.1 us
    dot_general x1, matrix products, per_device(): jnp.einsum('rf,df->rd', hidden_grad, back_up, preferred_element_type=jnp....  48.7 us
  transfers between devices with their start and end apart: 23, of which 13 were waited for; matrix products, arithmetic and copies ran while one was open for 44% of the time, Pallas kernels for 0%

profile of v1, /device:TPU:0, one launch (start us, length us, event | category | flops | bytes accessed | tf_op | source)
XLA Modules:
  0.0 1948.4 jit_solution(48368167901641121)
XLA Ops:
  28.3 43.7 %collective-permute-done = bf16[512,2048]{1,0:T(8,128)(2,1)S(1)} collective-permute-done((bf16[512,2048]{1,0:T(8,128)(2,1)}, bf16[512,2048]{1,0:T(8,128)(2,1)S(1)}, u32[]{:S(2)}, u32[]{:S(2)}) %collective-permute-start) | collective-permute-done | bytes 2097184 | tf_op jit(solution)/shard_map/ppermute | solution.py:97
  76.3 42.0 %collective-permute-done.2 = bf16[512,2048]{1,0:T(8,128)(2,1)} collective-permute-done((bf16[512,2048]{1,0:T(8,128)(2,1)S(1)}, bf16[512,2048]{1,0:T(8,128)(2,1)}, u32[]{:S(2)}, u32[]{:S(2)}) %collective-permute-start.2) | collective-permute-done | bytes 2097184 | tf_op jit(solution)/shard_map/ppermute | solution.py:97
  123.9 39.2 %collective-permute-done.4 = bf16[512,2048]{1,0:T(8,128)(2,1)} collective-permute-done((bf16[512,2048]{1,0:T(8,128)(2,1)}, bf16[512,2048]{1,0:T(8,128)(2,1)}, u32[]{:S(2)}, u32[]{:S(2)}) %collective-permute-start.4) | collective-permute-done | bytes 2097184 | tf_op jit(solution)/shard_map/ppermute | solution.py:97
  290.1 103.0 %while.44 = (s32[]{:T(128)}, bf16[8,512,4,64]{1,3,2,0:T(8,128)(2,1)S(1)}, f32[8,4,512]{2,1,0:T(4,128)S(1)}, s32[8]{0:T(128)S(1)}, bf16[4,1024,4,64]{1,3,2,0:T(8,...) while((s32[]{:T(128)}, ...), condition=%wide.region_5.6_spmd, body=%wide.region_2.5_spmd.sunk | while | flops 562558976 | bytes 29182452 | solution.py:144
  393.1 24.4 %fusion.81 = f32[4096,1024]{1,0:T(8,128)} fusion(bf16[4096,2048]{1,0:T(8,128)(2,1)} %constant_dynamic-update-slice_fusion, bf16[2048,1024]{1,0:T(8,128)(2,1)} %all-gather.17.cloned.1.call-done), kind=kOutput, calls=%fused_computation.144 | convolution fusion | flops 17179869184 | bytes 37748736 | tf_op jit(solution)/shard_map/dot_general | solution.py:113
  438.5 343.9 %while.46 = (s32[]{:T(128)}, f32[4,1024,4,64]{1,0,3,2:T(4,128)}, f32[4,1024,4,64]{1,0,3,2:T(4,128)}, bf16[4,1024,4,64]{1,3,2,0:T(8,128)(2,1)}, s32[4]{0:T(128)S(...) while((s32[]{:T(128)}, f32[4,1024,4,64]{1,0,3,2:T(4,128)}, ...), condition=%wide.region_11.12_spmd, body=%wide.region_7.11_spmd.sunk | while | flops 1375598592 | bytes 110209856 | solution.py:225
  444.2 33.4 %while.47 = (s32[]{:T(128)}, f32[1024,4,64]{0,2,1:T(8,128)S(1)}, f32[1024,4,64]{0,2,1:T(8,128)}, f32[2,512,4,64]{1,3,2,0:T(8,128)}, s32[2]{0:T(128)S(1)}, /*inde...) while((s32[]{:T(128)}, f32[1024,4,64]{0,2,1:T(8,128)S(1)}, ...), condition=%wide.region_10.10_spmd.clone, body=%wide.region_8.9_spmd.clone.sunk | while | flops 1375598592 | bytes 89196952 | solution.py:220
  484.8 20.0 %dynamic_update_slice.84 = f32[4,1024,4,64]{1,0,3,2:T(4,128)} dynamic-update-slice(f32[4,1024,4,64]{1,0,3,2:T(4,128)} %get-tuple-element.827, f32[1,1024,4,64]{1,0,3,2:T(1,128)S(1)} %copy.102, s32[]{:T(128)S(6)} %copy.143, s32[]{:T(128)} %constant.263.clone.1..sunk.1, s32[]{:T(128)} %constant.263.clone.1..sunk.1, s32[]{:T(128)} %constant.263.clone.1..sunk.1) | dynamic-update-slice | bytes 2097156 | tf_op jit(solution)/shard_map/while/body/jit(dynamic_update_index_in_dim)/dynamic_update_slice | solution.py:225
  504.8 20.0 %dynamic_update_slice.85 = f32[4,1024,4,64]{1,0,3,2:T(4,128)} dynamic-update-slice(f32[4,1024,4,64]{1,0,3,2:T(4,128)} %get-tuple-element.828, f32[1,1024,4,64]{1,0,3,2:T(1,128)S(1)} %copy-done, s32[]{:T(128)S(6)} %copy.143, s32[]{:T(128)} %constant.263.clone.1..sunk.1, s32[]{:T(128)} %constant.263.clone.1..sunk.1, s32[]{:T(128)} %constant.263.clone.1..sunk.1) | dynamic-update-slice | bytes 2097156 | tf_op jit(solution)/shard_map/while/body/jit(dynamic_update_index_in_dim)/dynamic_update_slice | solution.py:225
  530.2 33.4 %while.47 = (s32[]{:T(128)}, f32[1024,4,64]{0,2,1:T(8,128)S(1)}, f32[1024,4,64]{0,2,1:T(8,128)}, f32[2,512,4,64]{1,3,2,0:T(8,128)}, s32[2]{0:T(128)S(1)}, /*inde...) while((s32[]{:T(128)}, f32[1024,4,64]{0,2,1:T(8,128)S(1)}, ...), condition=%wide.region_10.10_spmd.clone, body=%wide.region_8.9_spmd.clone.sunk | while | flops 1375598592 | bytes 89196952 | solution.py:220
  570.8 19.9 %dynamic_update_slice.84 = f32[4,1024,4,64]{1,0,3,2:T(4,128)} dynamic-update-slice(f32[4,1024,4,64]{1,0,3,2:T(4,128)} %get-tuple-element.827, f32[1,1024,4,64]{1,0,3,2:T(1,128)S(1)} %copy.102, s32[]{:T(128)S(6)} %copy.143, s32[]{:T(128)} %constant.263.clone.1..sunk.1, s32[]{:T(128)} %constant.263.clone.1..sunk.1, s32[]{:T(128)} %constant.263.clone.1..sunk.1) | dynamic-update-slice | bytes 2097156 | tf_op jit(solution)/shard_map/while/body/jit(dynamic_update_index_in_dim)/dynamic_update_slice | solution.py:225
  590.7 20.0 %dynamic_update_slice.85 = f32[4,1024,4,64]{1,0,3,2:T(4,128)} dynamic-update-slice(f32[4,1024,4,64]{1,0,3,2:T(4,128)} %get-tuple-element.828, f32[1,1024,4,64]{1,0,3,2:T(1,128)S(1)} %copy-done, s32[]{:T(128)S(6)} %copy.143, s32[]{:T(128)} %constant.263.clone.1..sunk.1, s32[]{:T(128)} %constant.263.clone.1..sunk.1, s32[]{:T(128)} %constant.263.clone.1..sunk.1) | dynamic-update-slice | bytes 2097156 | tf_op jit(solution)/shard_map/while/body/jit(dynamic_update_index_in_dim)/dynamic_update_slice | solution.py:225
  615.9 33.4 %while.47 = (s32[]{:T(128)}, f32[1024,4,64]{0,2,1:T(8,128)S(1)}, f32[1024,4,64]{0,2,1:T(8,128)}, f32[2,512,4,64]{1,3,2,0:T(8,128)}, s32[2]{0:T(128)S(1)}, /*inde...) while((s32[]{:T(128)}, f32[1024,4,64]{0,2,1:T(8,128)S(1)}, ...), condition=%wide.region_10.10_spmd.clone, body=%wide.region_8.9_spmd.clone.sunk | while | flops 1375598592 | bytes 89196952 | solution.py:220
  656.6 19.9 %dynamic_update_slice.84 = f32[4,1024,4,64]{1,0,3,2:T(4,128)} dynamic-update-slice(f32[4,1024,4,64]{1,0,3,2:T(4,128)} %get-tuple-element.827, f32[1,1024,4,64]{1,0,3,2:T(1,128)S(1)} %copy.102, s32[]{:T(128)S(6)} %copy.143, s32[]{:T(128)} %constant.263.clone.1..sunk.1, s32[]{:T(128)} %constant.263.clone.1..sunk.1, s32[]{:T(128)} %constant.263.clone.1..sunk.1) | dynamic-update-slice | bytes 2097156 | tf_op jit(solution)/shard_map/while/body/jit(dynamic_update_index_in_dim)/dynamic_update_slice | solution.py:225
  676.5 20.0 %dynamic_update_slice.85 = f32[4,1024,4,64]{1,0,3,2:T(4,128)} dynamic-update-slice(f32[4,1024,4,64]{1,0,3,2:T(4,128)} %get-tuple-element.828, f32[1,1024,4,64]{1,0,3,2:T(1,128)S(1)} %copy-done, s32[]{:T(128)S(6)} %copy.143, s32[]{:T(128)} %constant.263.clone.1..sunk.1, s32[]{:T(128)} %constant.263.clone.1..sunk.1, s32[]{:T(128)} %constant.263.clone.1..sunk.1) | dynamic-update-slice | bytes 2097156 | tf_op jit(solution)/shard_map/while/body/jit(dynamic_update_index_in_dim)/dynamic_update_slice | solution.py:225
  701.7 33.4 %while.47 = (s32[]{:T(128)}, f32[1024,4,64]{0,2,1:T(8,128)S(1)}, f32[1024,4,64]{0,2,1:T(8,128)}, f32[2,512,4,64]{1,3,2,0:T(8,128)}, s32[2]{0:T(128)S(1)}, /*inde...) while((s32[]{:T(128)}, f32[1024,4,64]{0,2,1:T(8,128)S(1)}, ...), condition=%wide.region_10.10_spmd.clone, body=%wide.region_8.9_spmd.clone.sunk | while | flops 1375598592 | bytes 89196952 | solution.py:220
  742.4 19.9 %dynamic_update_slice.84 = f32[4,1024,4,64]{1,0,3,2:T(4,128)} dynamic-update-slice(f32[4,1024,4,64]{1,0,3,2:T(4,128)} %get-tuple-element.827, f32[1,1024,4,64]{1,0,3,2:T(1,128)S(1)} %copy.102, s32[]{:T(128)S(6)} %copy.143, s32[]{:T(128)} %constant.263.clone.1..sunk.1, s32[]{:T(128)} %constant.263.clone.1..sunk.1, s32[]{:T(128)} %constant.263.clone.1..sunk.1) | dynamic-update-slice | bytes 2097156 | tf_op jit(solution)/shard_map/while/body/jit(dynamic_update_index_in_dim)/dynamic_update_slice | solution.py:225
  762.3 20.0 %dynamic_update_slice.85 = f32[4,1024,4,64]{1,0,3,2:T(4,128)} dynamic-update-slice(f32[4,1024,4,64]{1,0,3,2:T(4,128)} %get-tuple-element.828, f32[1,1024,4,64]{1,0,3,2:T(1,128)S(1)} %copy-done, s32[]{:T(128)S(6)} %copy.143, s32[]{:T(128)} %constant.263.clone.1..sunk.1, s32[]{:T(128)} %constant.263.clone.1..sunk.1, s32[]{:T(128)} %constant.263.clone.1..sunk.1) | dynamic-update-slice | bytes 2097156 | tf_op jit(solution)/shard_map/while/body/jit(dynamic_update_index_in_dim)/dynamic_update_slice | solution.py:225
  840.5 36.3 %convert_reduce_fusion = (f32[1024]{0:T(1024)}, bf16[4096,1024]{1,0:T(8,128)(2,1)}) fusion(f32[4096,1024]{1,0:T(8,128)} %fusion.81, f32[1024]{0:T(1024)S(1)} %copy-done.46, bf16[4096,2048]{1,0:T(8,128)(2,1)} %all-gather.21.cloned.1.call-done, bf16[1024,2048]{1,0:T(8,128)(2,1)} %all-gather.19.cloned.1.call-done), kind=kOutput, calls=%fused_computation.68 | convolution fusion | flops 17276338176 | bytes 46145536 | tf_op jit(solution)/shard_map/rd,fd->rf/dot_general | solution.py:173
  876.8 48.7 %add_add_fusion = f32[4096,2048]{1,0:T(8,128)} fusion(f32[4096,2048]{1,0:T(8,128)} %fusion.84, f32[4096,2048]{1,0:T(8,128)} %fusion.82, f32[4096,2048]{1,0:T(8,128)} %fusion.83, bf16[4096,1024]{1,0:T(8,128)(2,1)} %get-tuple-element.433, bf16[2048,1024]{1,0:T(8,128)(2,1)} %all-gather.17.cloned.1.call-done), kind=kOutput, calls=%fused_computation.57 | convolution fusion | flops 17205035008 | bytes 146800640 | tf_op jit(solution)/shard_map/rf,df->rd/dot_general | solution.py:245
  943.6 34.0 %convolution_add_fusion = f32[4096,2048]{1,0:T(8,128)} fusion(f32[4096,2048]{1,0:T(8,128)} %fusion.80, bf16[1024,2048]{1,0:T(8,128)(2,1)S(1)} %copy-done.48, f32[4096,1024]{1,0:T(8,128)} %fusion.81, f32[1024]{0:T(1024)S(1)} %copy-done.46), kind=kOutput, calls=%fused_computation.60 | convolution fusion | flops 17230200832 | bytes 88084480 | tf_op jit(solution)/shard_map/dot_general | solution.py:150
  1025.0 24.2 %fusion.89 = f32[2048,1024]{1,0:T(8,128)} fusion(bf16[4096,2048]{1,0:T(8,128)(2,1)} %all-gather.23.cloned.1.call-done, bf16[4096,1024]{1,0:T(8,128)(2,1)} %get-tuple-element.433), kind=kOutput, calls=%fused_computation.152 | convolution fusion | flops 17179869184 | bytes 33554432 | tf_op jit(solution)/shard_map/rd,rf->df/dot_general | solution.py:240
  1049.2 28.8 %fusion.76 = f32[1024,2048]{1,0:T(8,128)} fusion(bf16[4096,2048]{1,0:T(8,128)(2,1)} %all-gather.21.cloned.1.call-done, f32[4096,1024]{1,0:T(8,128)} %fusion.81, f32[1024]{0:T(1024)S(1)} %copy-done.46), kind=kOutput, calls=%fused_computation.141 | convolution fusion | flops 17221812224 | bytes 41947136 | tf_op jit(solution)/shard_map/rf,rd->fd/dot_general | solution.py:169
  1081.0 15.2 all-reduce.1
  1096.2 183.7 %reduce-scatter.11.cloned.1.call-done = f32[512,2048]{1,0:T(8,128)} async-done(((f32[4096,2048]{1,0:T(8,128)}), f32[512,2048]{1,0:T(8,128)}) %reduce-scatter.11.cloned.1.call-update) | async-done | bytes 4194320 | tf_op jit(solution)/shard_map/reduce_scatter | solution.py:241
  1285.3 320.8 %reduce-scatter.9.cloned.1.call-done = f32[512,2048]{1,0:T(8,128)} async-done(((f32[4096,2048]{1,0:T(8,128)}), f32[512,2048]{1,0:T(8,128)}) %reduce-scatter.9.cloned.1.call-update) | async-done | bytes 4194320 | tf_op jit(solution)/shard_map/reduce_scatter | solution.py:148
  1613.7 38.3 %all-reduce = (f32[2048]{0:T(1024)}, f32[2048]{0:T(1024)}, f32[2048]{0:T(1024)S(1)}) all-reduce(f32[2048]{0:T(1024)S(1)} %get-tuple-element.359, f32[2048]{0:T(1024)S(1)} %get-tuple-element.361, f32[2048]{0:T(1024)S(1)} %get-tuple-element.460), channel_id=1, replica_groups=mesh['dp'=4,'tensor'=8] {'dp','tensor'}, use_global_device_ids=true, to_apply=%region_16.17 | all-reduce | flops 6144 | bytes 49152 | tf_op jit(solution)/shard_map/psum | solution.py:254
  1652.1 30.9 %reduce-scatter.19.cloned.1.call-done = f32[256,512]{1,0:T(8,128)} async-done(((f32[256,2048]{1,0:T(8,128)}), f32[256,512]{1,0:T(8,128)}) %reduce-scatter.19.cloned.1.call-update) | async-done | bytes 524304 | tf_op jit(solution)/shard_map/reduce_scatter | solution.py:278
  1682.9 38.8 %reduce-scatter.15.cloned.1.call-done = f32[512,256]{1,0:T(8,128)} async-done(((f32[2048,256]{1,0:T(8,128)}), f32[512,256]{1,0:T(8,128)}) %reduce-scatter.15.cloned.1.call-update) | async-done | bytes 524304 | tf_op jit(solution)/shard_map/reduce_scatter | solution.py:275
  1721.7 38.9 %reduce-scatter.13.cloned.1.call-done = f32[512,256]{1,0:T(8,128)} async-done(((f32[2048,256]{1,0:T(8,128)}), f32[512,256]{1,0:T(8,128)}) %reduce-scatter.13.cloned.1.call-update) | async-done | bytes 524304 | tf_op jit(solution)/shard_map/reduce_scatter | solution.py:274
  1760.6 89.9 %reduce-scatter.21.cloned.1.call-done = f32[512,1024]{1,0:T(8,128)} async-done(((f32[2048,1024]{1,0:T(8,128)}), f32[512,1024]{1,0:T(8,128)}) %reduce-scatter.21.cloned.1.call-update) | async-done | bytes 2097168 | tf_op jit(solution)/shard_map/reduce_scatter | solution.py:277
  1850.5 90.2 %reduce-scatter.23.cloned.1.call-done = f32[1024,512]{1,0:T(8,128)} async-done(((f32[1024,2048]{1,0:T(8,128)}), f32[1024,512]{1,0:T(8,128)}) %reduce-scatter.23.cloned.1.call-update) | async-done | bytes 2097168 | tf_op jit(solution)/shard_map/reduce_scatter | solution.py:279
  (494 shorter events, 554.0 us)
Async XLA Ops:
  7.2 185.1 %all-gather.13.cloned.1.call-start = ((), (), s32[]{:S(2)}) async-start(), calls=%async_computation.10 | async-start | bytes 1310720 | tf_op jit(solution)/shard_map/all_gather | solution.py:82
  7.9 214.8 %all-gather.11.cloned.1.call-start = ((), (), s32[]{:S(2)}) async-start(), calls=%async_computation.9 | async-start | bytes 1310720 | tf_op jit(solution)/shard_map/all_gather | solution.py:81
  8.7 244.5 %all-gather.9.cloned.1.call-start = ((), (), s32[]{:S(2)}) async-start(), calls=%async_computation.8 | async-start | bytes 1310720 | tf_op jit(solution)/shard_map/all_gather | solution.py:83
  9.4 383.7 %all-gather.17.cloned.1.call-start = ((), (), s32[]{:S(2)}) async-start(), calls=%async_computation.12 | async-start | bytes 5242880 | tf_op jit(solution)/shard_map/all_gather | solution.py:84
  10.0 407.5 %all-gather.15.cloned.1.call-start = ((), (), s32[]{:S(2)}) async-start(), calls=%async_computation.11 | async-start | bytes 1310720 | tf_op jit(solution)/shard_map/all_gather | solution.py:85
  10.6 406.9 %all-gather.21.cloned.1.call-start = ((), (), s32[]{:S(2)}) async-start(), calls=%async_computation.15 | async-start | bytes 18874368 | tf_op jit(solution)/shard_map/all_gather | solution.py:167
  11.2 829.4 %all-gather.19.cloned.1.call-start = ((), (), s32[]{:S(2)}) async-start(), calls=%async_computation.13 | async-start | bytes 5242880 | tf_op jit(solution)/shard_map/all_gather | solution.py:86
  11.9 965.8 %all-gather.23.cloned.1.call-start = ((), (), s32[]{:S(2)}) async-start(), calls=%async_computation.17 | async-start | bytes 18874368 | tf_op jit(solution)/shard_map/all_gather | solution.py:166
  15.7 107.5 %copy-start.51 = (bf16[256]{0:T(256)(128)(2,1)S(1)}, bf16[256]{0:T(256)(128)(2,1)}, u32[]{:S(2)}) copy-start(bf16[256]{0:T(256)(128)(2,1)} %param.32) | copy-start | bytes 1540
  15.8 107.5 %copy-start.47 = (bf16[1024]{0:T(1024)(128)(2,1)S(1)}, bf16[1024]{0:T(1024)(128)(2,1)}, u32[]{:S(2)}) copy-start(bf16[1024]{0:T(1024)(128)(2,1)} %param.36) | copy-start | bytes 6148
  23.8 48.2 %collective-permute-start = (bf16[512,2048]{1,0:T(8,128)(2,1)}, bf16[512,2048]{1,0:T(8,128)(2,1)S(1)}, u32[]{:S(2)}, u32[]{:S(2)}) collective-permute-start(bf16[512,2048]{1,0:T(8,128)(2,1)} %get-tuple-element.439), channel_id=1, source_target_pairs={{0,1},{1,2},{2,3},{3,4},{4,5},{5,6},{6,7},{7,0},{8,9},{9,10},{10,1... | collective-permute-start | bytes 6291464 | tf_op jit(solution)/shard_map/ppermute | solution.py:97
  24.2 48.4 %collective-permute-start.1 = (bf16[512,2048]{1,0:T(8,128)(2,1)}, bf16[512,2048]{1,0:T(8,128)(2,1)S(1)}, u32[]{:S(2)}, u32[]{:S(2)}) collective-permute-start(bf16[512,2048]{1,0:T(8,128)(2,1)} %get-tuple-element.439), channel_id=1, source_target_pairs={{0,7},{1,0},{2,1},{3,2},{4,3},{5,4},{6,5},{7,6},{8,15},{9,8},{10,9... | collective-permute-start | bytes 6291464 | tf_op jit(solution)/shard_map/ppermute | solution.py:104
  72.0 46.3 %collective-permute-start.2 = (bf16[512,2048]{1,0:T(8,128)(2,1)S(1)}, bf16[512,2048]{1,0:T(8,128)(2,1)}, u32[]{:S(2)}, u32[]{:S(2)}) collective-permute-start(bf16[512,2048]{1,0:T(8,128)(2,1)S(1)} %collective-permute-done), channel_id=1, source_target_pairs={{0,1},{1,2},{2,3},{3,4},{4,5},{5,6},{6,7},{7,0},{8,9},{9,10},{10,1... | collective-permute-start | bytes 6291464 | tf_op jit(solution)/shard_map/ppermute | solution.py:97
  72.6 46.5 %collective-permute-start.3 = (bf16[512,2048]{1,0:T(8,128)(2,1)S(1)}, bf16[512,2048]{1,0:T(8,128)(2,1)}, u32[]{:S(2)}, u32[]{:S(2)}) collective-permute-start(bf16[512,2048]{1,0:T(8,128)(2,1)S(1)} %collective-permute-done.1), channel_id=1, source_target_pairs={{0,7},{1,0},{2,1},{3,2},{4,3},{5,4},{6,5},{7,6},{8,15},{9,8},{10,9... | collective-permute-start | bytes 6291464 | tf_op jit(solution)/shard_map/ppermute | solution.py:104
  118.3 44.8 %collective-permute-start.4 = (bf16[512,2048]{1,0:T(8,128)(2,1)}, bf16[512,2048]{1,0:T(8,128)(2,1)}, u32[]{:S(2)}, u32[]{:S(2)}) collective-permute-start(bf16[512,2048]{1,0:T(8,128)(2,1)} %collective-permute-done.2), channel_id=1, source_target_pairs={{0,1},{1,2},{2,3},{3,4},{4,5},{5,6},{6,7},{7,0},{8,9},{9,10},{10,1... | collective-permute-start | bytes 6291464 | tf_op jit(solution)/shard_map/ppermute | solution.py:97
  119.1 57.5 %collective-permute-start.5 = (bf16[512,2048]{1,0:T(8,128)(2,1)}, bf16[512,2048]{1,0:T(8,128)(2,1)}, u32[]{:S(2)}, u32[]{:S(2)}) collective-permute-start(bf16[512,2048]{1,0:T(8,128)(2,1)} %collective-permute-done.3), channel_id=1, source_target_pairs={{0,7},{1,0},{2,1},{3,2},{4,3},{5,4},{6,5},{7,6},{8,15},{9,8},{10,9... | collective-permute-start | bytes 6291464 | tf_op jit(solution)/shard_map/ppermute | solution.py:104
  123.0 1156.9 %reduce-scatter.11.cloned.1.call-start = ((), (), s32[]{:S(2)}) async-start(), calls=%async_computation.16 | async-start | bytes 37748736 | tf_op jit(solution)/shard_map/reduce_scatter | solution.py:241
  163.1 27.7 %collective-permute-start.6 = (bf16[512,2048]{1,0:T(8,128)(2,1)}, bf16[512,2048]{1,0:T(8,128)(2,1)S(1)}, u32[]{:S(2)}, u32[]{:S(2)}) collective-permute-start(bf16[512,2048]{1,0:T(8,128)(2,1)} %collective-permute-done.4), channel_id=1, source_target_pairs={{0,1},{1,2},{2,3},{3,4},{4,5},{5,6},{6,7},{7,0},{8,9},{9,10},{10,1... | collective-permute-start | bytes 6291464 | tf_op jit(solution)/shard_map/ppermute | solution.py:97
  164.1 115.3 %copy-start.22 = (f32[1024,32]{0,1:T(8,128)}, f32[1024,32]{0,1:T(8,128)S(1)}, u32[]{:S(2)}) copy-start(f32[1024,32]{0,1:T(8,128)S(1)} %get-tuple-element.469) | copy-start | bytes 393220
  925.5 680.7 %reduce-scatter.9.cloned.1.call-start = ((), (), s32[]{:S(2)}) async-start(), calls=%async_computation.14 | async-start | bytes 37748736 | tf_op jit(solution)/shard_map/reduce_scatter | solution.py:148
  977.6 674.5 %reduce-scatter.17.cloned.1.call-start = ((), (), s32[]{:S(2)}) async-start(), calls=%async_computation.20 | async-start | bytes 2621440 | tf_op jit(solution)/shard_map/reduce_scatter | solution.py:276
  988.9 694.0 %reduce-scatter.19.cloned.1.call-start = ((), (), s32[]{:S(2)}) async-start(), calls=%async_computation.21 | async-start | bytes 2621440 | tf_op jit(solution)/shard_map/reduce_scatter | solution.py:278
  1001.7 720.0 %reduce-scatter.15.cloned.1.call-start = ((), (), s32[]{:S(2)}) async-start(), calls=%async_computation.19 | async-start | bytes 2621440 | tf_op jit(solution)/shard_map/reduce_scatter | solution.py:275
  1014.7 745.9 %reduce-scatter.13.cloned.1.call-start = ((), (), s32[]{:S(2)}) async-start(), calls=%async_computation.18 | async-start | bytes 2621440 | tf_op jit(solution)/shard_map/reduce_scatter | solution.py:274
  1024.7 825.8 %reduce-scatter.21.cloned.1.call-start = ((), (), s32[]{:S(2)}) async-start(), calls=%async_computation.22 | async-start | bytes 10485760 | tf_op jit(solution)/shard_map/reduce_scatter | solution.py:277
  1049.2 891.5 %reduce-scatter.23.cloned.1.call-start = ((), (), s32[]{:S(2)}) async-start(), calls=%async_computation.23 | async-start | bytes 10485760 | tf_op jit(solution)/shard_map/reduce_scatter | solution.py:279
  1078.1 201.8 %copy-start.2 = (bf16[512,2048]{1,0:T(8,128)(2,1)S(1)}, bf16[512,2048]{1,0:T(8,128)(2,1)}, u32[]{:S(2)}) copy-start(bf16[512,2048]{1,0:T(8,128)(2,1)} %param.23) | copy-start | bytes 6291460
  1078.1 201.8 %copy-start.30 = (f32[2048]{0:T(1024)S(1)}, f32[2048]{0:T(1024)}, u32[]{:S(2)}) copy-start(f32[2048]{0:T(1024)} %copy-done.29) | copy-start | bytes 24580
  1078.1 201.8 %copy-start.33 = (f32[512]{0:T(512)S(1)}, f32[512]{0:T(512)}, u32[]{:S(2)}) copy-start(f32[512]{0:T(512)} %copy-done.32) | copy-start | bytes 6148
  1078.7 204.5 %copy-start.37 = (f32[512]{0:T(512)S(1)}, f32[512]{0:T(512)}, u32[]{:S(2)}) copy-start(f32[512]{0:T(512)} %copy-done.36) | copy-start | bytes 6148
  1078.7 204.5 %copy-start.35 = (f32[512]{0:T(512)S(1)}, f32[512]{0:T(512)}, u32[]{:S(2)}) copy-start(f32[512]{0:T(512)} %copy-done.34) | copy-start | bytes 6148
  1652.0 289.3 %copy-start.40 = (f32[2048]{0:T(1024)}, f32[2048]{0:T(1024)S(1)}, u32[]{:S(2)}) copy-start(f32[2048]{0:T(1024)S(1)} %get-tuple-element.895) | copy-start | bytes 24580
  (74 other events, 679.2 us)
Sparse Core Ops, SparseCore 0:
  9.9 29.3 all-gather.12
  41.1 26.6 all-gather.10
  69.6 26.6 all-gather.8
  97.9 52.6 all-gather.16
  152.3 26.4 all-gather.14
  180.3 151.1 all-gather.20
  333.3 54.6 all-gather.18
  390.2 151.1 all-gather.22
  925.6 354.2 reduce-scatter.10
  1282.2 323.8 reduce-scatter.8
  1609.7 34.3 reduce-scatter.16
  1647.7 35.1 reduce-scatter.18
  1686.5 35.1 reduce-scatter.14
  1725.4 35.1 reduce-scatter.12
  1764.1 86.3 reduce-scatter.20
  1854.3 86.3 reduce-scatter.22
